TPU v7x, 32 devices: a whole 2x2x4 slice. The times are simulated.
32 devices in a mesh: groups: 2 (over x), month: 16 (over z, y, core).
Axes of the slice: x: 2, y: 2, z: 4, core: 2. Of those that a mesh axis runs over, the one named last changes fastest.
Arguments:
- shocks: float32 [512, 4096], P('month', 'groups'), parts along dimension 1, may hold values from -6 to 6
- long_mean: float32 [512], P('month'), may hold values from 0 to 0.08
- reversion: float32 [4096], P('groups'), parts along dimension 0, may hold values from 0.1 to 1
- volatility: float32 [4096], P('groups'), parts along dimension 0, may hold values from 0.004 to 0.015
- start_rate: float32 [4096], P('groups'), parts along dimension 0, may hold values from 0 to 0.06
- cash_flows: bfloat16 [3, 512, 24576], P(None, 'month', 'groups'), parts along dimension 2, may hold values from -0.5 to 0.5
Outputs:
- present: bfloat16 [3, 24576, 2048], P(None, ('groups', 'month')), parts along dimension 1
There are 2 independent parts, one for each index of `groups`. A program takes and returns all parts, laid end to end along the dimension named above; an argument that names none is the same for every part. Nothing has to cross between parts.
All inputs are finite; a program needn't handle non-finite values.
Results may differ from a plain program's by a relative error of at most 0.0049.
Values may be sent and summed in bfloat16 or wider, within the bound.
A program may use at most 192 MiB of HBM per device.

v0:
```python
import math

import jax
import jax.numpy as jnp
from jax import lax
from jax.sharding import PartitionSpec as P

month_step = 1.0 / 12.0
root_step = math.sqrt(1.0 / 12.0)
risk_price = 0.15
price_scale = risk_price * math.sqrt(12.0)
price_drift = 0.5 * risk_price * risk_price


def prefix(part, axis, combine, identity):
    place = lax.axis_index(axis)
    gathered = jax.tree.map(lambda a: lax.all_gather(a, axis), part)
    state = jax.tree.map(lambda a, e: jnp.zeros_like(a) + jnp.asarray(e, a.dtype), part, identity)

    def one(hop, state):
        return combine(
            state, jax.tree.map(lambda a: lax.dynamic_index_in_dim(a, hop, 0, False), gathered)
        )

    return lax.fori_loop(0, place, one, state)


def compose(earlier, later):
    return (
        later[0] * earlier[0],
        later[0] * earlier[1] + later[1],
        earlier[2] + later[2] * earlier[0],
        earlier[3] + later[3] + later[2] * earlier[1],
    )


def month_maps(shocks, long_mean, reversion, volatility):
    persist = 1.0 - reversion * month_step
    drive = (reversion * month_step)[None, :] * long_mean[:, None] + (volatility * root_step)[
        None, :
    ] * shocks
    factor = jnp.broadcast_to(persist[None, :], drive.shape)
    extra = drive + price_scale * shocks + price_drift
    return lax.associative_scan(compose, (factor, drive, factor, extra), axis=0)


def discount_from(maps, rate_in, total_in):
    total = total_in[None, :] + maps[2] * rate_in[None, :] + maps[3]
    return jnp.exp(-month_step * total).astype(jnp.bfloat16)


def time_discount(shocks, long_mean, reversion, volatility, start_rate):
    maps = month_maps(shocks, long_mean, reversion, volatility)
    block = tuple((member[-1] for member in maps))
    unit_row = jnp.ones_like(start_rate)
    zero_row = jnp.zeros_like(start_rate)
    before = prefix(block, "month", compose, (unit_row, zero_row, zero_row, zero_row))
    rate_in = before[0] * start_rate + before[1]
    total_in = before[2] * start_rate + before[3]
    return discount_from(maps, rate_in, total_in)


def contract(flows, discount):
    blocks = []
    for leg_index in range(flows.shape[0]):
        value = lax.dot_general(
            flows[leg_index], discount, (((0,), (0,)), ((), ())), preferred_element_type=jnp.float32
        )
        blocks.append(value.astype(jnp.bfloat16))
    return jnp.stack(blocks)


def local(shocks, long_mean, reversion, volatility, start_rate, cash_flows):
    own_flows = lax.all_to_all(cash_flows, "month", split_axis=2, concat_axis=1, tiled=True)
    discount = time_discount(shocks, long_mean, reversion, volatility, start_rate)
    every_month = lax.all_gather(discount, "month", axis=0, tiled=True)
    return contract(own_flows, every_month)


def solution(mesh):
    placed = (
        P("month", "groups"),
        P("month"),
        P("groups"),
        P("groups"),
        P("groups"),
        P(None, "month", "groups"),
    )
    return jax.shard_map(
        local,
        mesh=mesh,
        in_specs=placed,
        out_specs=P(None, ("groups", "month"), None),
        check_vma=False,
    )
```

profile of v0, /device:TPU:0, one launch (start us, length us, event | category | flops | bytes accessed | tf_op | source)
XLA Modules:
  0.0 273.4 jit_solution(5829222085009719674)
XLA Ops:
  6.5 15.3 %copy.13 = bf16[3,32,12288]{1,0,2:T(4,128)(2,1)} copy(bf16[3,32,12288]{2,1,0:T(8,128)(2,1)} %param.13) | data formatting | bytes 4718592 | tf_op args[5]
  21.8 15.7 %reshape.39 = bf16[16,2,36864]{2,1,0:T(2,128)(2,1)} reshape(bf16[12288,3,32]{2,1,0:T(4,128)(2,1)} %bitcast.69) | data formatting | bytes 4718592
  37.5 0.0 copy-start.2
  37.5 0.0 copy-start.3
  37.5 0.0 copy-start
  37.5 0.0 copy-start.4
  37.5 7.6 %all-to-all-start = ((bf16[16,2,36864]{2,1,0:T(2,128)(2,1)}), bf16[16,2,36864]{2,1,0:T(2,128)(2,1)S(1)}, u32[]{:S(2)}, u32[]{:S(2)}) async-start(bf16[16,2,36864]{2,1,0:T(2,128)(2,1)} %reshape.39), calls=%async_computation | async-start | bytes 4718592 | tf_op jit(solution)/shard_map/all_to_all | solution.py:74
  45.1 0.0 all-gather.6.cloned.1.call-start
  45.1 0.0 copy-done.2
  45.2 0.0 copy-done.3
  45.2 0.0 copy-done
  45.2 0.0 copy-done.4
  45.2 0.1 multiply_add_fusion.3
  45.4 0.6 slice.387
  46.0 0.1 slice.349
  46.2 0.6 slice.388
  46.9 0.6 slice.363
  48.1 0.1 fusion.21
  48.8 0.1 multiply_add_fusion.9
  49.2 0.6 add.336
  49.9 0.7 multiply_add_fusion.6
  50.6 0.7 pad_maximum_fusion.6
  51.3 0.7 pad_maximum_fusion.8
  52.2 0.7 add.363
  52.9 0.7 add.309
  53.5 0.7 add_multiply_fusion.1
  54.2 0.9 pad_maximum_fusion.7
  55.1 0.9 pad.153
  56.0 0.0 copy-start.1
  56.0 0.9 add_add_fusion.2
  57.1 43.2 %all-gather.2 = f32[16,1,2048]{2,1,0:T(1,128)S(1)} all-gather(f32[1,1,2048]{2,1,0:T(1,128)S(1)} %add_bitcast_fusion.1), channel_id=1, replica_groups=mesh['groups'=2,'month'=16] {'month'}, dimensions={0}, use_global_device_ids=true | all-gather | bytes 139264 | tf_op jit(solution)/shard_map/all_gather | solution.py:17
  100.3 0.7 copy.29
  101.0 0.7 pad_maximum_fusion.4
  101.8 1.0 pad.165
  102.8 28.5 %all-gather.3 = f32[16,1,2048]{2,1,0:T(1,128)S(1)} all-gather(f32[1,1,2048]{2,1,0:T(1,128)S(1)} %add_bitcast_fusion), channel_id=1, replica_groups=mesh['groups'=2,'month'=16] {'month'}, dimensions={0}, use_global_device_ids=true | all-gather | bytes 139264 | tf_op jit(solution)/shard_map/all_gather | solution.py:17
  131.3 0.7 copy.28
  132.0 2.3 pad.299
  134.4 1.4 pad.301
  135.8 0.9 add_bitcast_fusion.2
  136.7 17.8 %all-gather.1 = f32[16,1,2048]{2,1,0:T(1,128)S(1)} all-gather(f32[1,1,2048]{2,1,0:T(1,128)S(1)} %get-tuple-element.132), channel_id=1, replica_groups=mesh['groups'=2,'month'=16] {'month'}, dimensions={0}, use_global_device_ids=true | all-gather | bytes 139264 | tf_op jit(solution)/shard_map/all_gather | solution.py:17
  154.5 0.7 copy.30
  155.2 19.1 %all-gather = f32[16,1,2048]{2,1,0:T(1,128)S(1)} all-gather(f32[1,1,2048]{2,1,0:T(1,128)S(1)} %get-tuple-element.133), channel_id=1, replica_groups=mesh['groups'=2,'month'=16] {'month'}, dimensions={0}, use_global_device_ids=true | all-gather | bytes 139264 | tf_op jit(solution)/shard_map/all_gather | solution.py:17
  174.3 0.7 copy.31
  175.0 0.2 while.16
  175.2 0.0 copy-done.1
  175.2 0.7 exponential_convert_fusion
  175.9 0.0 all-gather.6.cloned.1.call-update
  176.0 0.0 all-to-all-done
  176.0 11.8 %reshape.40 = bf16[12288,3,32]{2,1,0:T(4,128)(2,1)} reshape(bf16[16,2,36864]{2,1,0:T(2,128)(2,1)S(1)} %all-to-all-done) | data formatting | bytes 4718592
  187.7 11.7 %copy.19 = bf16[3,32,16,768]{3,2,1,0:T(8,128)(2,1)S(1)} copy(bf16[3,32,16,768]{1,0,3,2:T(4,128)(2,1)} %bitcast.68) | data formatting | bytes 4718592 | tf_op jit(solution)/shard_map/all_to_all | solution.py:74
  199.4 0.2 fusion.18
  199.6 0.2 copy.15
  199.8 0.2 copy.17
  200.1 0.2 copy.16
  200.3 41.7 %all-gather.6.cloned.1.call-done = bf16[512,2048]{1,0:T(8,128)(2,1)} async-done(((bf16[32,2048]{1,0:T(8,128)(2,1)}), bf16[512,2048]{1,0:T(8,128)(2,1)}) %all-gather.6.cloned.1.call-update) | async-done | bytes 2097168 | tf_op jit(solution)/shard_map/all_gather | solution.py:76
  242.0 0.0 copy-start.5
  242.0 3.6 %fusion.1 = bf16[1,768,2048]{1,2,0:T(8,128)(2,1)S(1)} fusion(bf16[512,2048]{1,0:T(8,128)(2,1)} %all-gather.6.cloned.1.call-done, bf16[512,768]{1,0:T(8,128)(2,1)S(1)} %bitcast.77), kind=kOutput, calls=%fused_computation.12 | convolution fusion | flops 1612185600 | bytes 6029312 | tf_op jit(solution)/shard_map/dot_general | solution.py:66
  245.6 0.0 copy-done.5
  245.6 1.9 fusion.2
  247.5 1.9 fusion
  249.4 4.6 %pad_maximum_fusion = bf16[3,768,2048]{1,2,0:T(8,128)(2,1)} fusion(bf16[1,768,2048]{1,2,0:T(8,128)(2,1)S(1)} %fusion.2, bf16[1,768,2048]{1,2,0:T(8,128)(2,1)S(1)} %fusion.1, bf16[1,768,2048]{1,2,0:T(8,128)(2,1)S(1)} %fusion), kind=kLoop, calls=%fused_computation.7 | loop fusion | flops 9437184 | bytes 18874368 | tf_op jit(solution)/shard_map/stack | solution.py:70
  253.9 12.6 %copy.18 = bf16[3,768,2048]{2,1,0:T(8,128)(2,1)} copy(bf16[3,768,2048]{1,2,0:T(8,128)(2,1)} %pad_maximum_fusion) | data formatting | bytes 18874368 | tf_op jit(solution)/shard_map/stack | solution.py:70
  (85 shorter events, 2.0 us)
Async XLA Ops:
  37.5 7.6 %copy-start.2 = (f32[2048]{0:T(1024)S(1)}, f32[2048]{0:T(1024)}, u32[]{:S(2)}) copy-start(f32[2048]{0:T(1024)} %param.10) | copy-start | bytes 24580
  37.5 7.6 %copy-start.3 = (f32[2048]{0:T(1024)S(1)}, f32[2048]{0:T(1024)}, u32[]{:S(2)}) copy-start(f32[2048]{0:T(1024)} %param.11) | copy-start | bytes 24580
  37.5 7.7 %copy-start = (f32[32,2048]{1,0:T(8,128)S(1)}, f32[32,2048]{1,0:T(8,128)}, u32[]{:S(2)}) copy-start(f32[32,2048]{1,0:T(8,128)} %param.8) | copy-start | bytes 786436
  37.5 7.7 %copy-start.4 = (f32[32]{0:T(128)S(1)}, f32[32]{0:T(128)}, u32[]{:S(2)}) copy-start(f32[32]{0:T(128)} %param.9) | copy-start | bytes 388
  37.5 138.4 %all-to-all-start = ((bf16[16,2,36864]{2,1,0:T(2,128)(2,1)}), bf16[16,2,36864]{2,1,0:T(2,128)(2,1)S(1)}, u32[]{:S(2)}, u32[]{:S(2)}) async-start(bf16[16,2,36864]{2,1,0:T(2,128)(2,1)} %reshape.39), calls=%async_computation | async-start | bytes 4718592 | tf_op jit(solution)/shard_map/all_to_all | solution.py:74
  45.1 196.9 %all-gather.6.cloned.1.call-start = ((), (), s32[]{:S(2)}) async-start(), calls=%async_computation.1 | async-start | bytes 2228224 | tf_op jit(solution)/shard_map/all_gather | solution.py:76
  56.0 119.2 %copy-start.1 = (f32[2048]{0:T(1024)S(1)}, f32[2048]{0:T(1024)}, u32[]{:S(2)}) copy-start(f32[2048]{0:T(1024)} %param.12) | copy-start | bytes 24580
  242.0 3.6 %copy-start.5 = (bf16[512,2048]{1,0:T(8,128)(2,1)S(1)}, bf16[512,2048]{1,0:T(8,128)(2,1)}, u32[]{:S(2)}) copy-start(bf16[512,2048]{1,0:T(8,128)(2,1)} %all-gather.6.cloned.1.call-done) | copy-start | bytes 6291460
Sparse Core Ops, SparseCore 0:
  176.1 65.8 all-gather.5
where the time goes:
time: 277 us; the launch traced here: 273 us
  blocking collectives  109 us (39%)
  local copies, waits for them, and re-layouts  79.5 us (29%)
  waiting for transfers between devices  41.7 us (15%)
  other arithmetic  14.3 us (5%)
  between operations  14.1 us (5%)
  starting transfers between devices  7.6 us (3%)
  matrix products  7.31 us (3%)
    all_gather x4, blocking collectives, prefix(): gathered = jax.tree.map(lambda a: lax.all_gather(a, axis), part)  109 us
    unnamed x21, local copies, waits for them, and re-layouts  49.3 us
    all_gather x1, waiting for transfers between devices, local(): every_month = lax.all_gather(discount, 'month', axis=0, tiled=True)  41.7 us
    another operation x1, local copies, waits for them, and re-layouts, contract(): return jnp.stack(blocks)  12.6 us
    all_to_all x1, local copies, waits for them, and re-layouts, local(): lax.all_to_all(cash_flows, 'month', split_axis=2, concat_axis=1, tiled=True)  11.7 us
    all_to_all x1, starting transfers between devices, local(): lax.all_to_all(cash_flows, 'month', split_axis=2, concat_axis=1, tiled=True)  7.56 us
    dot_general x3, matrix products, contract(): lax.dot_general(flows[leg_index], discount, (((0,), (0,)), ((), ())), pre...  7.31 us
  transfers between devices with their start and end apart: 2, of which 1 were waited for; matrix products, arithmetic and copies ran while one was open for 17% of the time, Pallas kernels for 0%

commit v1 on v0

v1 whole, which is shorter than its diff:
```python
import functools
import math

import jax
import jax.numpy as jnp
from jax import lax
from jax.experimental import pallas as pl
from jax.experimental.pallas import tpu as pltpu
from jax.sharding import PartitionSpec as P

month_step = 1.0 / 12.0
root_step = math.sqrt(1.0 / 12.0)
risk_price = 0.15
price_scale = risk_price * math.sqrt(12.0)
price_drift = 0.5 * risk_price * risk_price
MESH = pl.DeviceIdType.MESH
CORES = 2


def kernel(
    n,
    sides,
    shocks,
    long_mean,
    reversion,
    volatility,
    start_rate,
    cash_flows,
    flows_out,
    discount_out,
    reach_ref,
    total_ref,
    part_ref,
    level_ref,
    block_ref,
    stage_ref,
    flow_send,
    flow_recv,
    part_send,
    part_recv,
    level_send,
    level_recv,
    up_send,
    up_recv,
    down_send,
    down_recv,
    side_send,
    side_recv,
    twin_send,
    twin_recv,
    own_sem,
):
    rows, width = shocks.shape
    legs = cash_flows.shape[0]
    own = cash_flows.shape[2] // n
    team = sides * CORES
    depth = n // team
    me = lax.axis_index("month")
    z, spot = me // team, me % team
    side, core = spot // CORES, spot % CORES
    place = lambda z, side, core: (z * sides + side) * CORES + core

    def remote(src, dst, send, recv, device):
        return pltpu.make_async_remote_copy(
            src_ref=src,
            dst_ref=dst,
            send_sem=send,
            recv_sem=recv,
            device_id={"month": device},
            device_id_type=MESH,
        )

    barrier = pltpu.get_barrier_semaphore()
    for k in range(1, n):
        pl.semaphore_signal(
            barrier, inc=1, device_id={"month": (me + k) % n}, device_id_type=MESH
        )
    stage = pltpu.make_async_copy(
        cash_flows.at[:, :, pl.ds(pl.multiple_of(me * own, own), own)], stage_ref, own_sem.at[0]
    )
    stage.start()
    pl.semaphore_wait(barrier, n - 1)

    stride = n // 2 - 1
    hops = [(i * stride) % n for i in range(1, n)]

    def flow_copy(slot, sender, receiver, device):
        leg = slot // (n - 1)
        return remote(
            cash_flows.at[leg, :, pl.ds(pl.multiple_of(receiver * own, own), own)],
            flows_out.at[pl.ds(pl.multiple_of(sender * rows, rows), rows), pl.ds(leg * own, own)],
            flow_send.at[slot],
            flow_recv.at[slot],
            device,
        )

    def flow_out(slot):
        to = (me + hops[slot % (n - 1)]) % n
        return flow_copy(slot, me, to, to)

    def flow_in(slot):
        source = (me + n - hops[slot % (n - 1)]) % n
        return flow_copy(slot, source, me, source)

    count = (n - 1) * legs
    fills = depth + 3
    started = [0]

    def fill(upto):
        for slot in range(started[0], min(count, upto)):
            flow_out(slot).start()
        started[0] = max(started[0], min(count, upto))

    share = -(-count // fills)
    fill(share)

    chunk = math.gcd(width, 512)
    unit = jnp.ones((1, chunk), jnp.float32)
    zero = jnp.zeros((1, chunk), jnp.float32)
    last = []
    for c in range(width // chunk):
        lanes = pl.ds(c * chunk, chunk)
        pull = reversion[lanes].reshape(1, chunk) * month_step
        sway = volatility[lanes].reshape(1, chunk) * root_step
        persist = 1.0 - pull

        def month(t, carry):
            rate, power, reach, total = carry
            shock = shocks[pl.ds(t, 1), lanes]
            rate = persist * rate + (pull * long_mean[t] + sway * shock)
            power = persist * power
            reach = reach + power
            total = total + (rate + price_scale * shock + price_drift)
            reach_ref[pl.ds(t, 1), lanes] = reach
            total_ref[pl.ds(t, 1), lanes] = total
            return rate, power, reach, total

        rate, power, reach, total = lax.fori_loop(
            0, rows, month, (zero, unit, zero, zero), unroll=4
        )
        part_ref[spot, 0:1, lanes] = rate
        part_ref[spot, 1:2, lanes] = total
        last.append((power, reach))
    power = jnp.concatenate([one[0] for one in last], axis=1)
    reach = jnp.concatenate([one[1] for one in last], axis=1)

    def part_copy(k, slot, device):
        return remote(
            part_ref.at[slot], part_ref.at[slot], part_send.at[k], part_recv.at[k], device
        )

    for k in range(1, team):
        part_copy(k, spot, z * team + (spot + k) % team).start()
    fill(2 * share)
    for k in range(1, team):
        source = (spot + team - k) % team
        part_copy(k, source, z * team + source).wait_recv()

    rate, total = part_ref[0, 0:1], part_ref[0, 1:2]
    level_power, level_reach = power, reach
    for j in range(1, team):
        rate, total = (
            power * rate + part_ref[j, 0:1],
            total + reach * rate + part_ref[j, 1:2],
        )
        level_reach = level_reach + reach * level_power
        level_power = power * level_power
    level_ref[z, 0:1] = rate
    level_ref[z, 1:2] = total

    def level_copy(k, slot, device):
        return remote(
            level_ref.at[slot], level_ref.at[slot], level_send.at[k], level_recv.at[k], device
        )

    for k in range(1, depth):

        @pl.when(z + k < depth)
        def _():
            level_copy(k, z, place(z + k, side, core)).start()

    fill(3 * share)

    for k in range(1, depth):

        @pl.when(z - k >= 0)
        def _():
            level_copy(k, z - k, place(z - k, side, core)).wait_recv()

    def past_level(j, state):
        rate, total = state
        return (
            level_power * rate + level_ref[j, 0:1],
            total + level_reach * rate + level_ref[j, 1:2],
        )

    def past_part(j, state):
        rate, total = state
        return power * rate + part_ref[j, 0:1], total + reach * rate + part_ref[j, 1:2]

    state = (start_rate[...].reshape(1, width), jnp.zeros((1, width), jnp.float32))
    state = lax.fori_loop(0, z, past_level, state)
    rate, total = lax.fori_loop(0, spot, past_part, state)
    exponent = total + reach_ref[...] * rate + total_ref[...]
    block_ref[...] = jnp.exp(-month_step * exponent).astype(jnp.bfloat16)

    def months(m):
        return discount_out.at[pl.ds(pl.multiple_of(m * rows, rows), rows)]

    waits = []

    def send(cond, make):
        waits.append((cond, make))
        if cond is None:
            make().start()
        else:
            pl.when(cond)(lambda: make().start())

    def up_copy(h, shard, src, device):
        return remote(src, months(shard), up_send.at[h], up_recv.at[h], device)

    def down_copy(h, shard, src, device):
        return remote(src, months(shard), down_send.at[h], down_recv.at[h], device)

    def side_copy(level, shard, src, device):
        return remote(src, months(shard), side_send.at[level], side_recv.at[level], device)

    def twin_copy(level, lane, shard, src, device):
        slot = level * sides + lane
        return remote(src, months(shard), twin_send.at[slot], twin_recv.at[slot], device)

    def beside(cond, level, src):
        shard = place(level, side, core)
        if sides > 1:
            send(cond, lambda: side_copy(level, shard, src, place(z, 1 - side, core)))
        send(cond, lambda: twin_copy(level, side, shard, src, place(z, side, 1 - core)))

    def across(cond, level):
        shard = place(level, 1 - side, core)

        def take():
            side_copy(level, shard, months(shard), place(z, 1 - side, core)).wait_recv()

        if cond is None:
            take()
        else:
            pl.when(cond)(take)
        send(
            cond,
            lambda: twin_copy(
                level, 1 - side, shard, months(shard), place(z, side, 1 - core)
            ),
        )

    keep = pltpu.make_async_copy(block_ref, months(me), own_sem.at[1])
    keep.start()
    send(z + 1 < depth, lambda: up_copy(0, me, block_ref, place(z + 1, side, core)))
    send(z > 0, lambda: down_copy(0, me, block_ref, place(z - 1, side, core)))
    beside(None, z, block_ref)
    fill(4 * share)
    for h in range(1, depth):
        low, high = place(z - h, side, core), place(z + h, side, core)

        @pl.when(z - h >= 0)
        def _():
            up_copy(h - 1, low, months(low), place(z - 1, side, core)).wait_recv()

        send(
            (z - h >= 0) & (z + 1 < depth),
            lambda h=h, low=low: up_copy(h, low, months(low), place(z + 1, side, core)),
        )

        @pl.when(z + h < depth)
        def _():
            down_copy(h - 1, high, months(high), place(z + 1, side, core)).wait_recv()

        send(
            (z + h < depth) & (z > 0),
            lambda h=h, high=high: down_copy(h, high, months(high), place(z - 1, side, core)),
        )
        beside(z - h >= 0, z - h, months(low))
        beside(z + h < depth, z + h, months(high))
        if sides > 1:
            if h == 1:
                across(None, z)
            else:
                across(z - h + 1 >= 0, z - h + 1)
                across(z + h - 1 < depth, z + h - 1)
        fill((4 + h) * share)
    if sides > 1:
        if depth == 1:
            across(None, z)
        else:
            across(z - depth + 1 >= 0, z - depth + 1)
            across(z + depth - 1 < depth, z + depth - 1)
    fill(count)

    stage.wait()
    for leg in range(legs):
        pltpu.make_async_copy(
            stage_ref.at[leg],
            flows_out.at[pl.ds(pl.multiple_of(me * rows, rows), rows), pl.ds(leg * own, own)],
            own_sem.at[2 + leg],
        ).start()
    for level in range(depth):
        for lane in range(sides):
            shard = place(level, lane, 1 - core)
            twin_copy(level, lane, shard, months(shard), place(z, side, 1 - core)).wait_recv()
    for slot in range(count):
        flow_in(slot).wait_recv()
    for leg in range(legs):
        pltpu.make_async_copy(
            stage_ref.at[leg],
            flows_out.at[pl.ds(pl.multiple_of(me * rows, rows), rows), pl.ds(leg * own, own)],
            own_sem.at[2 + leg],
        ).wait()
    keep.wait()
    for k in range(1, team):
        part_copy(k, spot, z * team + (spot + k) % team).wait_send()
    for k in range(1, depth):

        @pl.when(z + k < depth)
        def _():
            level_copy(k, z, place(z + k, side, core)).wait_send()

    for cond, make in waits:
        if cond is None:
            make().wait_send()
        else:
            pl.when(cond)(lambda make=make: make().wait_send())
    for slot in range(count):
        flow_out(slot).wait_send()


def local(n, sides, shocks, long_mean, reversion, volatility, start_rate, cash_flows):
    rows, width = shocks.shape
    legs, _, cells = cash_flows.shape
    own = cells // n
    team = sides * CORES
    depth = n // team
    count = (n - 1) * legs
    dma = pltpu.SemaphoreType.DMA
    vmem = pl.BlockSpec(memory_space=pltpu.VMEM)
    anywhere = pl.BlockSpec(memory_space=pl.ANY)
    flows, discount = pl.pallas_call(
        functools.partial(kernel, n, sides),
        out_shape=(
            jax.ShapeDtypeStruct((n * rows, legs * own), jnp.bfloat16),
            jax.ShapeDtypeStruct((n * rows, width), jnp.bfloat16),
        ),
        in_specs=[vmem, pl.BlockSpec(memory_space=pltpu.SMEM), vmem, vmem, vmem, anywhere],
        out_specs=(anywhere, anywhere),
        scratch_shapes=[
            pltpu.VMEM((rows, width), jnp.float32),
            pltpu.VMEM((rows, width), jnp.float32),
            pltpu.VMEM((team, 2, width), jnp.float32),
            pltpu.VMEM((depth, 2, width), jnp.float32),
            pltpu.VMEM((rows, width), jnp.bfloat16),
            pltpu.VMEM((legs, rows, own), jnp.bfloat16),
            dma((count,)),
            dma((count,)),
            dma((team,)),
            dma((team,)),
            dma((depth,)),
            dma((depth,)),
            dma((depth,)),
            dma((depth,)),
            dma((depth,)),
            dma((depth,)),
            dma((depth,)),
            dma((depth,)),
            dma((n // CORES,)),
            dma((n // CORES,)),
            dma((2 + legs,)),
        ],
        compiler_params=pltpu.CompilerParams(collective_id=0, has_side_effects=True),
        name="exchange",
    )(shocks, long_mean, reversion, volatility, start_rate, cash_flows)
    value = lax.dot_general(
        flows, discount, (((0,), (0,)), ((), ())), preferred_element_type=jnp.float32
    )
    return value.astype(jnp.bfloat16).reshape(legs, own, width)


def solution(mesh):
    n = mesh.shape["month"]
    sides = max(1, 4 // mesh.shape["groups"])
    placed = (
        P("month", "groups"),
        P("month"),
        P("groups"),
        P("groups"),
        P("groups"),
        P(None, "month", "groups"),
    )
    return jax.shard_map(
        functools.partial(local, n, sides),
        mesh=mesh,
        in_specs=placed,
        out_specs=P(None, ("groups", "month"), None),
        check_vma=False,
    )
```

time: 277 us -> 80.7 us (0.29); the launches traced: 273 us -> 80.5 us
  blocking collectives: 109 us -> 0 us
  local copies, waits for them, and re-layouts: 79.5 us -> 0 us
  Pallas kernels: 0 us -> 71 us
  waiting for transfers between devices: 41.7 us -> 0 us
  other arithmetic: 14.3 us -> 0 us
  between operations: 14.1 us -> 0.01 us
  starting transfers between devices: 7.6 us -> 0 us
    all_gather x4 -> x0, blocking collectives: 109 us -> none  [prefix(): gathered = jax.tree.map(lambda a: lax.all_gather(a, axis), part)]
    pallas_call x0 -> x1, Pallas kernels: none -> 71 us  [local(): pl.pallas_call(functools.partial(kernel, n, sides), out_shape=(jax.ShapeD...]
    unnamed x21 -> x0, local copies, waits for them, and re-layouts: 49.3 us -> none
    all_gather x1 -> x0, waiting for transfers between devices: 41.7 us -> none  [local(): every_month = lax.all_gather(discount, 'month', axis=0, tiled=True)]
    another operation x2 -> x0, local copies, waits for them, and re-layouts: 12.6 us -> none  [the longest x1 12.6 us: contract(): return jnp.stack(blocks)]
    all_to_all x1 -> x0, local copies, waits for them, and re-layouts: 11.7 us -> none  [local(): lax.all_to_all(cash_flows, 'month', split_axis=2, concat_axis=1, tiled=True)]
    all_to_all x1 -> x0, starting transfers between devices: 7.56 us -> none  [local(): lax.all_to_all(cash_flows, 'month', split_axis=2, concat_axis=1, tiled=True)]
    another operation x1 -> x0, other arithmetic: 4.59 us -> none  [contract(): return jnp.stack(blocks)]
  transfers between devices with their start and end apart: 2 -> 0, of which waited for: 1 -> 0; matrix products, arithmetic and copies ran while one was open for 17% -> 0% of each run, Pallas kernels for 0% -> 0%
where the time goes in v1:
time: 80.7 us; the launch traced here: 80.5 us
  Pallas kernels  71 us (88%)
  matrix products  9.52 us (12%)
    pallas_call x1, Pallas kernels, local(): pl.pallas_call(functools.partial(kernel, n, sides), out_shape=(jax.ShapeD...  71 us
    dot_general x1, matrix products, local(): lax.dot_general(flows, discount, (((0,), (0,)), ((), ())), preferred_elem...  9.52 us

profile of v1, /device:TPU:0, one launch (start us, length us, event | category | flops | bytes accessed | tf_op | source)
XLA Modules:
  0.0 80.5 jit_solution(10957829999281894542)
XLA Ops:
  0.0 71.0 %exchange.1 = (bf16[512,2304]{1,0:T(8,128)(2,1)}, bf16[512,2048]{1,0:T(8,128)(2,1)}) custom-call(f32[32,2048]{1,0:T(8,128)} %shocks.1, f32[32]{0:T(128)} %long_mean.1, f32[2048]{0:T(1024)} %reversion.1, f32[2048]{0:T(1024)} %volatility.1, f32[2048]{0:T(1024)} %start_rate.1, bf16[3,32,12288]{2,1,0:T(8,128)(2,1)} %cash_flows.1), custom_call_target="tpu_custom_call" | custom-call | tf_op jit(solution)/shard_map/exchange/pallas_call | solution.py:345
  71.0 9.5 %convolution_convert_fusion = bf16[2304,2048]{1,0:T(8,128)(2,1)} fusion(bf16[512,2304]{1,0:T(8,128)(2,1)} %get-tuple-element.7, bf16[512,2048]{1,0:T(8,128)(2,1)} %get-tuple-element.8), kind=kOutput, calls=%fused_computation | convolution fusion | flops 4836556800 | bytes 13893632 | tf_op jit(solution)/shard_map/dot_general | solution.py:379

commit v2 on v1

--- a/solution.py
+++ b/solution.py
@@ -15,6 +15,51 @@
 price_drift = 0.5 * risk_price * risk_price
 MESH = pl.DeviceIdType.MESH
 CORES = 2
+VMEM_BYTES = 67_043_328
+SLACK = 65536
+
+
+def product(flows, discount, first, cells, out, row, after=None):
+    width = discount.shape[1]
+    tall, wide = math.gcd(cells, 256), math.gcd(width, 1024)
+    for tile in range(cells // tall):
+        for c in range(width // wide):
+            cols = pl.ds(c * wide, wide)
+            value = lax.dot_general(
+                flows[:, pl.ds(first + tile * tall, tall)],
+                discount[:, cols],
+                (((0,), (0,)), ((), ())),
+                preferred_element_type=jnp.float32,
+            )
+            out[pl.ds(row + tile * tall, tall), cols] = value.astype(jnp.bfloat16)
+        if after is not None:
+            after(tile, tall)
+
+
+def finish(flows, discount, done, out, last, sems):
+    cells = last.shape[0]
+    ready, width = done.shape
+    parts = ready // cells
+
+    def ship(k):
+        rows = pl.ds(k * cells, cells)
+        return pltpu.make_async_copy(done.at[rows], out.at[rows], sems.at[k])
+
+    def tail(tile, tall):
+        return pltpu.make_async_copy(
+            last.at[pl.ds(tile * tall, tall)],
+            out.at[pl.ds(ready + tile * tall, tall)],
+            sems.at[parts + tile],
+        )
+
+    for k in range(parts):
+        ship(k).start()
+    product(flows, discount, ready, cells, last, 0, lambda tile, tall: tail(tile, tall).start())
+    for k in range(parts):
+        ship(k).wait()
+    tall = math.gcd(cells, 256)
+    for tile in range(cells // tall):
+        tail(tile, tall).wait()
 
 
 def kernel(
@@ -28,12 +73,11 @@
     cash_flows,
     flows_out,
     discount_out,
+    done_out,
     reach_ref,
     total_ref,
     part_ref,
     level_ref,
-    block_ref,
-    stage_ref,
     flow_send,
     flow_recv,
     part_send,
@@ -75,10 +119,15 @@
         pl.semaphore_signal(
             barrier, inc=1, device_id={"month": (me + k) % n}, device_id_type=MESH
         )
-    stage = pltpu.make_async_copy(
-        cash_flows.at[:, :, pl.ds(pl.multiple_of(me * own, own), own)], stage_ref, own_sem.at[0]
-    )
-    stage.start()
+    def keep(leg):
+        return pltpu.make_async_copy(
+            cash_flows.at[leg, :, pl.ds(pl.multiple_of(me * own, own), own)],
+            flows_out.at[pl.ds(pl.multiple_of(me * rows, rows), rows), pl.ds(leg * own, own)],
+            own_sem.at[leg],
+        )
+
+    for leg in range(legs):
+        keep(leg).start()
     pl.semaphore_wait(barrier, n - 1)
 
     stride = n // 2 - 1
@@ -103,7 +152,7 @@
         return flow_copy(slot, source, me, source)
 
     count = (n - 1) * legs
-    fills = depth + 3
+    fills = depth + 8
     started = [0]
 
     def fill(upto):
@@ -202,7 +251,9 @@
     state = lax.fori_loop(0, z, past_level, state)
     rate, total = lax.fori_loop(0, spot, past_part, state)
     exponent = total + reach_ref[...] * rate + total_ref[...]
-    block_ref[...] = jnp.exp(-month_step * exponent).astype(jnp.bfloat16)
+    discount_out[pl.ds(pl.multiple_of(me * rows, rows), rows), :] = jnp.exp(
+        -month_step * exponent
+    ).astype(jnp.bfloat16)
 
     def months(m):
         return discount_out.at[pl.ds(pl.multiple_of(m * rows, rows), rows)]
@@ -252,11 +303,9 @@
             ),
         )
 
-    keep = pltpu.make_async_copy(block_ref, months(me), own_sem.at[1])
-    keep.start()
-    send(z + 1 < depth, lambda: up_copy(0, me, block_ref, place(z + 1, side, core)))
-    send(z > 0, lambda: down_copy(0, me, block_ref, place(z - 1, side, core)))
-    beside(None, z, block_ref)
+    send(z + 1 < depth, lambda: up_copy(0, me, months(me), place(z + 1, side, core)))
+    send(z > 0, lambda: down_copy(0, me, months(me), place(z - 1, side, core)))
+    beside(None, z, months(me))
     fill(4 * share)
     for h in range(1, depth):
         low, high = place(z - h, side, core), place(z + h, side, core)
@@ -295,26 +344,16 @@
             across(z + depth - 1 < depth, z + depth - 1)
     fill(count)
 
-    stage.wait()
-    for leg in range(legs):
-        pltpu.make_async_copy(
-            stage_ref.at[leg],
-            flows_out.at[pl.ds(pl.multiple_of(me * rows, rows), rows), pl.ds(leg * own, own)],
-            own_sem.at[2 + leg],
-        ).start()
     for level in range(depth):
         for lane in range(sides):
             shard = place(level, lane, 1 - core)
             twin_copy(level, lane, shard, months(shard), place(z, side, 1 - core)).wait_recv()
-    for slot in range(count):
-        flow_in(slot).wait_recv()
     for leg in range(legs):
-        pltpu.make_async_copy(
-            stage_ref.at[leg],
-            flows_out.at[pl.ds(pl.multiple_of(me * rows, rows), rows), pl.ds(leg * own, own)],
-            own_sem.at[2 + leg],
-        ).wait()
-    keep.wait()
+        for slot in range(leg * (n - 1), (leg + 1) * (n - 1)):
+            flow_in(slot).wait_recv()
+        keep(leg).wait()
+        if leg < legs - 1:
+            product(flows_out, discount_out, leg * own, own, done_out, leg * own)
     for k in range(1, team):
         part_copy(k, spot, z * team + (spot + k) % team).wait_send()
     for k in range(1, depth):
@@ -339,24 +378,24 @@
     team = sides * CORES
     depth = n // team
     count = (n - 1) * legs
+    held = 2 * (n * rows * (legs * own + width) + (legs - 1) * own * width) + SLACK
     dma = pltpu.SemaphoreType.DMA
     vmem = pl.BlockSpec(memory_space=pltpu.VMEM)
-    anywhere = pl.BlockSpec(memory_space=pl.ANY)
-    flows, discount = pl.pallas_call(
+    anywhere = pl.BlockSpec(memory_space=pltpu.HBM)
+    flows, discount, done = pl.pallas_call(
         functools.partial(kernel, n, sides),
         out_shape=(
-            jax.ShapeDtypeStruct((n * rows, legs * own), jnp.bfloat16),
-            jax.ShapeDtypeStruct((n * rows, width), jnp.bfloat16),
+            pltpu.VMEM((n * rows, legs * own), jnp.bfloat16),
+            pltpu.VMEM((n * rows, width), jnp.bfloat16),
+            pltpu.VMEM(((legs - 1) * own, width), jnp.bfloat16),
         ),
         in_specs=[vmem, pl.BlockSpec(memory_space=pltpu.SMEM), vmem, vmem, vmem, anywhere],
-        out_specs=(anywhere, anywhere),
+        out_specs=(vmem, vmem, vmem),
         scratch_shapes=[
             pltpu.VMEM((rows, width), jnp.float32),
             pltpu.VMEM((rows, width), jnp.float32),
             pltpu.VMEM((team, 2, width), jnp.float32),
             pltpu.VMEM((depth, 2, width), jnp.float32),
-            pltpu.VMEM((rows, width), jnp.bfloat16),
-            pltpu.VMEM((legs, rows, own), jnp.bfloat16),
             dma((count,)),
             dma((count,)),
             dma((team,)),
@@ -371,15 +410,27 @@
             dma((depth,)),
             dma((n // CORES,)),
             dma((n // CORES,)),
-            dma((2 + legs,)),
+            dma((legs,)),
         ],
-        compiler_params=pltpu.CompilerParams(collective_id=0, has_side_effects=True),
+        compiler_params=pltpu.CompilerParams(
+            collective_id=0, has_side_effects=True, vmem_limit_bytes=VMEM_BYTES - held
+        ),
         name="exchange",
     )(shocks, long_mean, reversion, volatility, start_rate, cash_flows)
-    value = lax.dot_general(
-        flows, discount, (((0,), (0,)), ((), ())), preferred_element_type=jnp.float32
-    )
-    return value.astype(jnp.bfloat16).reshape(legs, own, width)
+    tiles = own // math.gcd(own, 256)
+    present = pl.pallas_call(
+        finish,
+        out_shape=jax.ShapeDtypeStruct((legs * own, width), jnp.bfloat16),
+        in_specs=[vmem, vmem, vmem],
+        out_specs=anywhere,
+        scratch_shapes=[
+            pltpu.VMEM((own, width), jnp.bfloat16),
+            dma((legs - 1 + tiles,)),
+        ],
+        compiler_params=pltpu.CompilerParams(vmem_limit_bytes=16 << 20),
+        name="finish",
+    )(flows, discount, done)
+    return present.reshape(legs, own, width)
 
 
 def solution(mesh):

time: 80.7 us -> 74 us (0.917)
  matrix products: 9.52 us -> 0 us
  Pallas kernels: 71 us -> 73.5 us
    dot_general x1 -> x0, matrix products: 9.52 us -> none  [local(): lax.dot_general(flows, discount, (((0,), (0,)), ((), ())), preferred_elem...]
    pallas_call x1 -> x2, Pallas kernels: 71 us -> 73.5 us  [the longest x1 69.8 us: local(): pl.pallas_call(functools.partial(kernel, n, sides), out_shape=(pltpu.VMEM...]
where the time goes in v2:
time: 74 us; the launch traced here: 73.5 us
  Pallas kernels  73.5 us (99%)
    pallas_call x1, Pallas kernels, local(): pl.pallas_call(functools.partial(kernel, n, sides), out_shape=(pltpu.VMEM...  69.8 us
    pallas_call x1, Pallas kernels, local(): pl.pallas_call(finish, out_shape=jax.ShapeDtypeStruct((legs * own, width)...  3.72 us

profile of v2, /device:TPU:0, one launch (start us, length us, event | category | flops | bytes accessed | tf_op | source)
XLA Modules:
  0.0 73.5 jit_solution(15998581991871517882)
XLA Ops:
  0.0 69.8 %exchange.1 = (bf16[512,2304]{1,0:T(8,128)(2,1)S(1)}, bf16[512,2048]{1,0:T(8,128)(2,1)S(1)}, bf16[1536,2048]{1,0:T(8,128)(2,1)S(1)}) custom-call(f32[32,2048]{1,0:T(8,128)} %shocks.1, f32[32]{0:T(128)} %long_mean.1, f32[2048]{0:T(1024)} %reversion.1, f32[2048]{0:T(1024)} %volatility.1, f32[2048]{0:T(1024)} %start_rate.1, bf16[3,32,12288]{2,1,0:T(8,128)(2,1)} %cash_flows.1), custom_call_target="tpu_custom_call" | custom-call | tf_op jit(solution)/shard_map/exchange/pallas_call | solution.py:385
  69.8 3.7 %finish.1 = bf16[2304,2048]{1,0:T(8,128)(2,1)} custom-call(bf16[512,2304]{1,0:T(8,128)(2,1)S(1)} %get-tuple-element.8.flows, bf16[512,2048]{1,0:T(8,128)(2,1)S(1)} %get-tuple-element.9.discount, bf16[1536,2048]{1,0:T(8,128)(2,1)S(1)} %get-tuple-element.10.done), custom_call_target="tpu_custom_call" | custom-call | tf_op jit(solution)/shard_map/finish/pallas_call | solution.py:421

commit v3 on v2

--- a/solution.py
+++ b/solution.py
@@ -128,7 +128,6 @@
 
     for leg in range(legs):
         keep(leg).start()
-    pl.semaphore_wait(barrier, n - 1)
 
     stride = n // 2 - 1
     hops = [(i * stride) % n for i in range(1, n)]
@@ -161,7 +160,7 @@
         started[0] = max(started[0], min(count, upto))
 
     share = -(-count // fills)
-    fill(share)
+    lead = 3 * share
 
     chunk = math.gcd(width, 512)
     unit = jnp.ones((1, chunk), jnp.float32)
@@ -193,6 +192,8 @@
     power = jnp.concatenate([one[0] for one in last], axis=1)
     reach = jnp.concatenate([one[1] for one in last], axis=1)
 
+    pl.semaphore_wait(barrier, n - 1)
+
     def part_copy(k, slot, device):
         return remote(
             part_ref.at[slot], part_ref.at[slot], part_send.at[k], part_recv.at[k], device
@@ -214,42 +215,36 @@
         )
         level_reach = level_reach + reach * level_power
         level_power = power * level_power
-    level_ref[z, 0:1] = rate
-    level_ref[z, 1:2] = total
-
-    def level_copy(k, slot, device):
+
+    def level_copy(device):
         return remote(
-            level_ref.at[slot], level_ref.at[slot], level_send.at[k], level_recv.at[k], device
-        )
-
-    for k in range(1, depth):
-
-        @pl.when(z + k < depth)
-        def _():
-            level_copy(k, z, place(z + k, side, core)).start()
-
-    fill(3 * share)
-
-    for k in range(1, depth):
-
-        @pl.when(z - k >= 0)
-        def _():
-            level_copy(k, z - k, place(z - k, side, core)).wait_recv()
-
-    def past_level(j, state):
-        rate, total = state
-        return (
-            level_power * rate + level_ref[j, 0:1],
-            total + level_reach * rate + level_ref[j, 1:2],
-        )
+            level_ref.at[1], level_ref.at[0], level_send.at[0], level_recv.at[0], device
+        )
+
+    fill(lead)
+
+    @pl.when(z == 0)
+    def _():
+        level_ref[0, 0:1] = start_rate[...].reshape(1, width)
+        level_ref[0, 1:2] = jnp.zeros((1, width), jnp.float32)
+
+    @pl.when(z > 0)
+    def _():
+        level_copy(place(z - 1, side, core)).wait_recv()
+
+    first_rate, first_total = level_ref[0, 0:1], level_ref[0, 1:2]
+
+    @pl.when(z + 1 < depth)
+    def _():
+        level_ref[1, 0:1] = level_power * first_rate + rate
+        level_ref[1, 1:2] = first_total + level_reach * first_rate + total
+        level_copy(place(z + 1, side, core)).start()
 
     def past_part(j, state):
         rate, total = state
         return power * rate + part_ref[j, 0:1], total + reach * rate + part_ref[j, 1:2]
 
-    state = (start_rate[...].reshape(1, width), jnp.zeros((1, width), jnp.float32))
-    state = lax.fori_loop(0, z, past_level, state)
-    rate, total = lax.fori_loop(0, spot, past_part, state)
+    rate, total = lax.fori_loop(0, spot, past_part, (first_rate, first_total))
     exponent = total + reach_ref[...] * rate + total_ref[...]
     discount_out[pl.ds(pl.multiple_of(me * rows, rows), rows), :] = jnp.exp(
         -month_step * exponent
@@ -306,7 +301,7 @@
     send(z + 1 < depth, lambda: up_copy(0, me, months(me), place(z + 1, side, core)))
     send(z > 0, lambda: down_copy(0, me, months(me), place(z - 1, side, core)))
     beside(None, z, months(me))
-    fill(4 * share)
+    fill(lead + share)
     for h in range(1, depth):
         low, high = place(z - h, side, core), place(z + h, side, core)
 
@@ -335,7 +330,7 @@
             else:
                 across(z - h + 1 >= 0, z - h + 1)
                 across(z + h - 1 < depth, z + h - 1)
-        fill((4 + h) * share)
+        fill(lead + (1 + h) * share)
     if sides > 1:
         if depth == 1:
             across(None, z)
@@ -356,11 +351,9 @@
             product(flows_out, discount_out, leg * own, own, done_out, leg * own)
     for k in range(1, team):
         part_copy(k, spot, z * team + (spot + k) % team).wait_send()
-    for k in range(1, depth):
-
-        @pl.when(z + k < depth)
-        def _():
-            level_copy(k, z, place(z + k, side, core)).wait_send()
+    @pl.when(z + 1 < depth)
+    def _():
+        level_copy(place(z + 1, side, core)).wait_send()
 
     for cond, make in waits:
         if cond is None:
@@ -395,13 +388,13 @@
             pltpu.VMEM((rows, width), jnp.float32),
             pltpu.VMEM((rows, width), jnp.float32),
             pltpu.VMEM((team, 2, width), jnp.float32),
-            pltpu.VMEM((depth, 2, width), jnp.float32),
+            pltpu.VMEM((2, 2, width), jnp.float32),
             dma((count,)),
             dma((count,)),
             dma((team,)),
             dma((team,)),
-            dma((depth,)),
-            dma((depth,)),
+            dma((1,)),
+            dma((1,)),
             dma((depth,)),
             dma((depth,)),
             dma((depth,)),

time: 74 us -> 74 us (level)
  the two profiles are of different devices: /device:TPU:0 before, /device:TPU:1 now
where the time goes in v3:
time: 74 us; the launch traced here: 73.9 us
  Pallas kernels  73.9 us (100%)
    pallas_call x1, Pallas kernels, local(): pl.pallas_call(functools.partial(kernel, n, sides), out_shape=(pltpu.VMEM...  70.2 us
    pallas_call x1, Pallas kernels, local(): pl.pallas_call(finish, out_shape=jax.ShapeDtypeStruct((legs * own, width)...  3.72 us

profile of v3, /device:TPU:1, one launch (start us, length us, event | category | flops | bytes accessed | tf_op | source)
XLA Modules:
  0.0 73.9 jit_solution(4133511607535678949)
XLA Ops:
  0.0 70.2 %exchange.1 = (bf16[512,2304]{1,0:T(8,128)(2,1)S(1)}, bf16[512,2048]{1,0:T(8,128)(2,1)S(1)}, bf16[1536,2048]{1,0:T(8,128)(2,1)S(1)}) custom-call(f32[32,2048]{1,0:T(8,128)} %shocks.1, f32[32]{0:T(128)} %long_mean.1, f32[2048]{0:T(1024)} %reversion.1, f32[2048]{0:T(1024)} %volatility.1, f32[2048]{0:T(1024)} %start_rate.1, bf16[3,32,12288]{2,1,0:T(8,128)(2,1)} %cash_flows.1), custom_call_target="tpu_custom_call" | custom-call | tf_op jit(solution)/shard_map/exchange/pallas_call | solution.py:378
  70.2 3.7 %finish.1 = bf16[2304,2048]{1,0:T(8,128)(2,1)} custom-call(bf16[512,2304]{1,0:T(8,128)(2,1)S(1)} %get-tuple-element.8.flows, bf16[512,2048]{1,0:T(8,128)(2,1)S(1)} %get-tuple-element.9.discount, bf16[1536,2048]{1,0:T(8,128)(2,1)S(1)} %get-tuple-element.10.done), custom_call_target="tpu_custom_call" | custom-call | tf_op jit(solution)/shard_map/finish/pallas_call | solution.py:414
